TPU v7x, 32 devices: a whole 2x2x4 slice. The times are simulated.
32 devices in a mesh: kpt: 2 (over y), pert: 4 (over z), pw: 4 (over x, core).
Axes of the slice: x: 2, y: 2, z: 4, core: 2. Of those that a mesh axis runs over, the one named last changes fastest.
Arguments:
- occupied: bfloat16 [3072, 8192], P(('kpt', 'pert'), 'pw'), parts along dimension 0, may hold values from -0.0625 to 0.0625
- response: bfloat16 [8, 128, 8192], P(('kpt', 'pert'), None, 'pw'), parts along dimension 0, may hold values from -6 to 6
Outputs:
- correlation: float32 [8, 128, 1536], P(('kpt', 'pert')), parts along dimension 0
- projected: float32 [8, 128, 8192], P(('kpt', 'pert'), None, 'pw'), parts along dimension 0
There are 2 independent parts, one for each index of `kpt`. A program takes and returns all parts, laid end to end along the dimension named above; each array names one. Nothing has to cross between parts.
All inputs are finite; a program needn't handle non-finite values.
Results may differ from a plain program's by a relative error of at most 0.00096.
Values may be sent and summed in bfloat16 or wider, within the bound.
No kernel may reach another device: no remote copies, remote signals or barrier semaphores. Data moves between devices by JAX's collectives and lax.ppermute only.
A program may use at most 64 MiB of HBM per device.

v0:
```python
import jax
import jax.numpy as jnp
from jax import lax
from jax.sharding import PartitionSpec as P


def from_behind(block, axis, distance):
    devices = range(lax.axis_size(axis))
    route = [((i - distance) % len(devices), i) for i in devices]
    return lax.ppermute(block, axis, route)


def local(occupied, response):
    rows = response.reshape(-1, response.shape[-1])
    band_local = occupied.shape[0]
    cycle_size = lax.axis_size("pert")
    total_bands = band_local * cycle_size
    zero_index = jnp.zeros((), jnp.int32)
    empty_correlation = jnp.zeros((rows.shape[0], total_bands), jnp.float32)
    empty_correction = jnp.zeros(rows.shape, jnp.float32)
    position = lax.axis_index("pert")

    def visit(step, piece, correlation, correction):
        owner = (position - step) % cycle_size
        start = owner * band_local
        part = lax.dot_general(
            rows, piece, (((1,), (1,)), ((), ())), preferred_element_type=jnp.float32
        )
        summed = lax.psum(part, "pw")
        correlation = lax.dynamic_update_slice(correlation, summed, (zero_index, start))
        correction = correction + jnp.dot(
            summed.astype(jnp.bfloat16), piece, preferred_element_type=jnp.float32
        )
        return (correlation, correction)

    def turn(step, state):
        piece, correlation, correction = state
        correlation, correction = visit(step, piece, correlation, correction)
        piece = from_behind(piece, "pert", 1)
        return (piece, correlation, correction)

    piece, correlation, correction = lax.fori_loop(
        0, cycle_size - 1, turn, (occupied, empty_correlation, empty_correction)
    )
    correlation, correction = visit(cycle_size - 1, piece, correlation, correction)
    projected = rows.astype(jnp.float32) - correction
    correlation_out = correlation.reshape(response.shape[0], response.shape[1], total_bands)
    return (correlation_out, projected.reshape(response.shape))


def solution(mesh):
    in_specs = (P(("kpt", "pert"), "pw"), P(("kpt", "pert"), None, "pw"))
    out_specs = (P(("kpt", "pert"), None, None), P(("kpt", "pert"), None, "pw"))
    return jax.shard_map(local, mesh=mesh, in_specs=in_specs, out_specs=out_specs, check_vma=False)
```

profile of v0, /device:TPU:0, one launch (start us, length us, event | category | flops | bytes accessed | tf_op | source)
XLA Modules:
  0.0 176.5 jit_solution(3041188094833959325)
XLA Ops:
  8.0 0.0 copy-start
  8.0 1.0 broadcast_in_dim.6
  9.0 0.7 copy-done
  9.7 120.9 %while.20 = (s32[]{:T(128)}, bf16[384,2048]{1,0:T(8,128)(2,1)S(1)}, f32[128,1536]{1,0:T(8,128)}, f32[128,2048]{1,0:T(8,128)}, bf16[128,2048]{1,0:T(8,128)(2,1)},...) while((s32[]{:T(128)}, bf16[384,2048]{1,0:T(8,128)(2,1)S(1)}, ...), condition=%wide.region_2.3_spmd.clone, body=%wide.region_0.2_spmd.clone.sunk | while | flops 403275776 | bytes 19267988 | solution.py:42
  9.7 0.0 all-reduce.5.cloned.1.call-start
  9.7 0.0 copy-start.2
  9.7 0.2 copy.12
  9.9 3.1 %collective-permute-start = (bf16[384,2048]{1,0:T(8,128)(2,1)S(1)}, bf16[384,2048]{1,0:T(8,128)(2,1)S(1)}, u32[]{:S(2)}, u32[]{:S(2)}) collective-permute-start(bf16[384,2048]{1,0:T(8,128)(2,1)S(1)} %copy.12), channel_id=1, source_target_pairs={{12,0},{0,4},{4,8},{8,12},{13,1},{1,5},{5,9},{9,13},{14,2},{2,6},{... | collective-permute-start | bytes 4718600 | tf_op jit(solution)/shard_map/while/body/eval_jaxpr/ppermute | solution.py:10
  13.0 0.0 copy-done.2
  13.0 1.3 fusion.20
  14.3 0.0 all-reduce.5.cloned.1.call-update
  14.3 33.2 %all-reduce.5.cloned.1.call-done = f32[128,384]{1,0:T(8,128)} async-done(((f32[128,384]{1,0:T(8,128)}), f32[128,384]{1,0:T(8,128)}) %all-reduce.5.cloned.1.call-update) | async-done | bytes 196624 | tf_op jit(solution)/shard_map/while/body/eval_jaxpr/psum | solution.py:29
  47.6 1.6 constant_dynamic-update-slice_fusion.3
  49.2 2.3 %convolution_add_fusion.3 = f32[128,2048]{1,0:T(8,128)} fusion(bf16[384,2048]{1,0:T(8,128)(2,1)S(1)} %copy.12, f32[128,2048]{1,0:T(8,128)} %get-tuple-element.247, pred[]{:T(512)S(6)} %compare.5, f32[128,384]{1,0:T(8,128)} %all-reduce.5.cloned.1.call-done), kind=kOutput, calls=%fused_computation.clone.1 | convolution fusion | flops 201900032 | bytes 3866625 | tf_op jit(solution)/shard_map/while/body/eval_jaxpr/dot_general | solution.py:31
  51.5 0.0 collective-permute-done
  51.5 0.0 all-reduce.5.cloned.1.call-start
  51.5 0.0 copy-start.2
  51.5 0.2 copy.12
  51.7 1.5 collective-permute-start
  53.2 0.0 copy-done.2
  53.2 1.3 fusion.20
  54.5 0.0 all-reduce.5.cloned.1.call-update
  54.6 32.1 %all-reduce.5.cloned.1.call-done = f32[128,384]{1,0:T(8,128)} async-done(((f32[128,384]{1,0:T(8,128)}), f32[128,384]{1,0:T(8,128)}) %all-reduce.5.cloned.1.call-update) | async-done | bytes 196624 | tf_op jit(solution)/shard_map/while/body/eval_jaxpr/psum | solution.py:29
  86.7 1.6 constant_dynamic-update-slice_fusion.3
  88.3 2.8 %convolution_add_fusion.3 = f32[128,2048]{1,0:T(8,128)} fusion(bf16[384,2048]{1,0:T(8,128)(2,1)S(1)} %copy.12, f32[128,2048]{1,0:T(8,128)} %get-tuple-element.247, pred[]{:T(512)S(6)} %compare.5, f32[128,384]{1,0:T(8,128)} %all-reduce.5.cloned.1.call-done), kind=kOutput, calls=%fused_computation.clone.1 | convolution fusion | flops 201900032 | bytes 3866625 | tf_op jit(solution)/shard_map/while/body/eval_jaxpr/dot_general | solution.py:31
  91.1 0.0 collective-permute-done
  91.1 0.0 all-reduce.5.cloned.1.call-start
  91.1 0.0 copy-start.2
  91.1 0.2 copy.12
  91.3 1.5 collective-permute-start
  92.8 0.0 copy-done.2
  92.8 1.3 fusion.20
  94.1 0.0 all-reduce.5.cloned.1.call-update
  94.2 32.1 %all-reduce.5.cloned.1.call-done = f32[128,384]{1,0:T(8,128)} async-done(((f32[128,384]{1,0:T(8,128)}), f32[128,384]{1,0:T(8,128)}) %all-reduce.5.cloned.1.call-update) | async-done | bytes 196624 | tf_op jit(solution)/shard_map/while/body/eval_jaxpr/psum | solution.py:29
  126.3 1.6 constant_dynamic-update-slice_fusion.3
  127.9 2.8 %convolution_add_fusion.3 = f32[128,2048]{1,0:T(8,128)} fusion(bf16[384,2048]{1,0:T(8,128)(2,1)S(1)} %copy.12, f32[128,2048]{1,0:T(8,128)} %get-tuple-element.247, pred[]{:T(512)S(6)} %compare.5, f32[128,384]{1,0:T(8,128)} %all-reduce.5.cloned.1.call-done), kind=kOutput, calls=%fused_computation.clone.1 | convolution fusion | flops 201900032 | bytes 3866625 | tf_op jit(solution)/shard_map/while/body/eval_jaxpr/dot_general | solution.py:31
  130.6 0.0 collective-permute-done
  130.6 0.0 all-reduce.3.cloned.1.call-start
  130.6 0.0 copy-start.1
  130.6 0.0 copy-start.3
  130.7 2.4 %convolution_bitcast_fusion = f32[128,384]{0,1:T(8,128)} fusion(bf16[384,2048]{1,0:T(8,128)(2,1)S(1)} %get-tuple-element.160, bf16[1,128,2048]{2,1,0:T(8,128)(2,1)} %bitcast.22), kind=kOutput, calls=%fused_computation.6 | convolution fusion | flops 201326592 | bytes 2293760 | tf_op jit(solution)/shard_map/dot_general | solution.py:26
  133.1 0.0 all-reduce.3.cloned.1.call-update
  133.1 32.1 %all-reduce.3.cloned.1.call-done = f32[128,384]{0,1:T(8,128)} async-done(((f32[128,384]{0,1:T(8,128)}), f32[128,384]{0,1:T(8,128)}) %all-reduce.3.cloned.1.call-update) | async-done | bytes 196624 | tf_op jit(solution)/shard_map/psum | solution.py:29
  165.3 1.1 copy.4
  166.3 0.7 constant_dynamic-update-slice_fusion.1
  167.0 0.0 copy-done.1
  167.0 0.0 copy-done.3
  167.0 2.4 %fusion.2 = f32[1,128,2048]{2,1,0:T(8,128)} fusion(f32[128,2048]{1,0:T(8,128)S(1)} %copy-done.1, bf16[384,2048]{1,0:T(8,128)(2,1)S(1)} %get-tuple-element.160, f32[128,384]{0,1:T(8,128)} %all-reduce.3.cloned.1.call-done, bf16[1,128,2048]{2,1,0:T(8,128)(2,1)S(1)} %bitcast.23), kind=kOutput, calls=%fused_computation.5 | convolution fusion | flops 202162176 | bytes 4390912 | tf_op jit(solution)/shard_map/dot_general | solution.py:31
  (1 shorter events, 0.0 us)
Async XLA Ops:
  8.0 1.7 copy-start
  9.7 37.9 %all-reduce.5.cloned.1.call-start = ((), (), s32[]{:S(2)}) async-start(), calls=%async_computation.1 | async-start | bytes 393216 | tf_op jit(solution)/shard_map/while/body/eval_jaxpr/psum | solution.py:29
  9.7 3.3 %copy-start.2 = (bf16[128,2048]{1,0:T(8,128)(2,1)S(1)}, bf16[128,2048]{1,0:T(8,128)(2,1)}, u32[]{:S(2)}) copy-start(bf16[128,2048]{1,0:T(8,128)(2,1)} %get-tuple-element.260) | copy-start | bytes 1572868 | tf_op jit(solution)/shard_map/while
  9.9 41.7 %collective-permute-start = (bf16[384,2048]{1,0:T(8,128)(2,1)S(1)}, bf16[384,2048]{1,0:T(8,128)(2,1)S(1)}, u32[]{:S(2)}, u32[]{:S(2)}) collective-permute-start(bf16[384,2048]{1,0:T(8,128)(2,1)S(1)} %copy.12), channel_id=1, source_target_pairs={{12,0},{0,4},{4,8},{8,12},{13,1},{1,5},{5,9},{9,13},{14,2},{2,6},{... | collective-permute-start | bytes 4718600 | tf_op jit(solution)/shard_map/while/body/eval_jaxpr/ppermute | solution.py:10
  51.5 35.2 %all-reduce.5.cloned.1.call-start = ((), (), s32[]{:S(2)}) async-start(), calls=%async_computation.1 | async-start | bytes 393216 | tf_op jit(solution)/shard_map/while/body/eval_jaxpr/psum | solution.py:29
  51.5 1.7 copy-start.2
  51.7 39.4 %collective-permute-start = (bf16[384,2048]{1,0:T(8,128)(2,1)S(1)}, bf16[384,2048]{1,0:T(8,128)(2,1)S(1)}, u32[]{:S(2)}, u32[]{:S(2)}) collective-permute-start(bf16[384,2048]{1,0:T(8,128)(2,1)S(1)} %copy.12), channel_id=1, source_target_pairs={{12,0},{0,4},{4,8},{8,12},{13,1},{1,5},{5,9},{9,13},{14,2},{2,6},{... | collective-permute-start | bytes 4718600 | tf_op jit(solution)/shard_map/while/body/eval_jaxpr/ppermute | solution.py:10
  91.1 35.2 %all-reduce.5.cloned.1.call-start = ((), (), s32[]{:S(2)}) async-start(), calls=%async_computation.1 | async-start | bytes 393216 | tf_op jit(solution)/shard_map/while/body/eval_jaxpr/psum | solution.py:29
  91.1 1.7 copy-start.2
  91.3 39.4 %collective-permute-start = (bf16[384,2048]{1,0:T(8,128)(2,1)S(1)}, bf16[384,2048]{1,0:T(8,128)(2,1)S(1)}, u32[]{:S(2)}, u32[]{:S(2)}) collective-permute-start(bf16[384,2048]{1,0:T(8,128)(2,1)S(1)} %copy.12), channel_id=1, source_target_pairs={{12,0},{0,4},{4,8},{8,12},{13,1},{1,5},{5,9},{9,13},{14,2},{2,6},{... | collective-permute-start | bytes 4718600 | tf_op jit(solution)/shard_map/while/body/eval_jaxpr/ppermute | solution.py:10
  130.6 34.6 %all-reduce.3.cloned.1.call-start = ((), (), s32[]{:S(2)}) async-start(), calls=%async_computation | async-start | bytes 393216 | tf_op jit(solution)/shard_map/psum | solution.py:29
  130.6 36.4 %copy-start.1 = (f32[128,2048]{1,0:T(8,128)S(1)}, f32[128,2048]{1,0:T(8,128)}, u32[]{:S(2)}) copy-start(f32[128,2048]{1,0:T(8,128)} %get-tuple-element.161) | copy-start | bytes 3145732
  130.6 36.4 %copy-start.3 = (bf16[128,2048]{1,0:T(8,128)(2,1)S(1)}, bf16[128,2048]{1,0:T(8,128)(2,1)}, u32[]{:S(2)}) copy-start(bf16[128,2048]{1,0:T(8,128)(2,1)} %get-tuple-element.272) | copy-start | bytes 1572868
Sparse Core Ops, SparseCore 0:
  14.4 33.0 all-reduce.4
  54.7 31.9 all-reduce.4
  94.2 31.9 all-reduce.4
Sparse Core Ops, SparseCore 1:
  133.4 31.8 all-reduce.2
where the time goes:
time: 177 us
  waiting for transfers between devices  130 us (73%)
  matrix products  16.5 us (9%)
  between operations  15.2 us (9%)
  local copies, waits for them, and re-layouts  8.78 us (5%)
  starting transfers between devices  6.19 us (3%)
    psum x4, waiting for transfers between devices, visit(): summed = lax.psum(part, 'pw')  130 us
    dot_general x4, matrix products, visit(): jnp.dot(summed.astype(jnp.bfloat16), piece, preferred_element_type=jnp.fl...  10.2 us
    dot_general x4, matrix products, visit(): lax.dot_general(rows, piece, (((1,), (1,)), ((), ())), preferred_element_...  6.32 us
    ppermute x3, starting transfers between devices, from_behind(): return lax.ppermute(block, axis, route)  6.18 us
    dynamic_update_slice x4, local copies, waits for them, and re-layouts, visit(): lax.dynamic_update_slice(correlation, summed, (zero_index, start))  5.54 us
  transfers between devices with their start and end apart: 7, of which 4 were waited for; matrix products, arithmetic and copies ran while one was open for 9% of the time, Pallas kernels for 0%

commit v1 on v0

--- a/solution.py
+++ b/solution.py
@@ -26,7 +26,8 @@
         part = lax.dot_general(
             rows, piece, (((1,), (1,)), ((), ())), preferred_element_type=jnp.float32
         )
-        summed = lax.psum(part, "pw")
+        parts = lax.all_gather(part, "pw", axis=0, tiled=False)
+        summed = parts.sum(axis=0)
         correlation = lax.dynamic_update_slice(correlation, summed, (zero_index, start))
         correction = correction + jnp.dot(
             summed.astype(jnp.bfloat16), piece, preferred_element_type=jnp.float32

time: 177 us -> 134 us (0.76)
  waiting for transfers between devices: 130 us -> 65.9 us
  blocking collectives: 0 us -> 35.5 us
  between operations: 15.2 us -> 0.69 us
  other arithmetic: 0.01 us -> 5.18 us
  starting transfers between devices: 6.19 us -> 3.22 us
  matrix products: 16.5 us -> 14.7 us
    psum x4 -> x0, waiting for transfers between devices: 130 us -> none  [visit(): summed = lax.psum(part, 'pw')]
    ppermute x3, waiting for transfers between devices: 0.01 us -> 65.9 us  [from_behind(): return lax.ppermute(block, axis, route)]
    all_gather x0 -> x4, blocking collectives: none -> 35.5 us  [visit(): parts = lax.all_gather(part, 'pw', axis=0, tiled=False)]
    reduce_sum x0 -> x4, other arithmetic: none -> 5.18 us  [visit(): summed = parts.sum(axis=0)]
    ppermute x3, starting transfers between devices: 6.18 us -> 3.22 us  [from_behind(): return lax.ppermute(block, axis, route)]
    dynamic_update_slice x4, local copies, waits for them, and re-layouts: 5.54 us -> 2.79 us  [visit(): lax.dynamic_update_slice(correlation, summed, (zero_index, start))]
    all_gather x0 -> x1, local copies, waits for them, and re-layouts: none -> 2.41 us  [visit(): parts = lax.all_gather(part, 'pw', axis=0, tiled=False)]
    dot_general x4, matrix products: 10.2 us -> 8.13 us  [visit(): jnp.dot(summed.astype(jnp.bfloat16), piece, preferred_element_type=jnp.fl...]
  transfers between devices with their start and end apart: 7 -> 3, of which waited for: 4 -> 3; matrix products, arithmetic and copies ran while one was open for 9% -> 13% of each run, Pallas kernels for 0% -> 0%
where the time goes in v1:
time: 134 us; the launch traced here: 133 us
  waiting for transfers between devices  65.9 us (49%)
  blocking collectives  35.5 us (26%)
  matrix products  14.7 us (11%)
  local copies, waits for them, and re-layouts  7.49 us (6%)
  other arithmetic  5.18 us (4%)
  starting transfers between devices  3.22 us (2%)
    ppermute x3, waiting for transfers between devices, from_behind(): return lax.ppermute(block, axis, route)  65.9 us
    all_gather x4, blocking collectives, visit(): parts = lax.all_gather(part, 'pw', axis=0, tiled=False)  35.5 us
    dot_general x4, matrix products, visit(): jnp.dot(summed.astype(jnp.bfloat16), piece, preferred_element_type=jnp.fl...  8.13 us
    dot_general x4, matrix products, visit(): lax.dot_general(rows, piece, (((1,), (1,)), ((), ())), preferred_element_...  6.53 us
    reduce_sum x4, other arithmetic, visit(): summed = parts.sum(axis=0)  5.18 us
    ppermute x3, starting transfers between devices, from_behind(): return lax.ppermute(block, axis, route)  3.22 us
    dynamic_update_slice x4, local copies, waits for them, and re-layouts, visit(): lax.dynamic_update_slice(correlation, summed, (zero_index, start))  2.79 us
  transfers between devices with their start and end apart: 3, of which 3 were waited for; matrix products, arithmetic and copies ran while one was open for 13% of the time, Pallas kernels for 0%

profile of v1, /device:TPU:0, one launch (start us, length us, event | category | flops | bytes accessed | tf_op | source)
XLA Modules:
  0.0 132.9 jit_solution(18235110073751850690)
XLA Ops:
  0.6 0.0 copy-start
  0.7 1.0 broadcast_in_dim.6
  1.6 0.7 copy-done
  2.3 114.0 %while.20 = (s32[]{:T(128)}, bf16[384,2048]{1,0:T(8,128)(2,1)S(1)}, f32[128,1536]{1,0:T(8,128)}, f32[128,2048]{1,0:T(8,128)}, bf16[128,2048]{1,0:T(8,128)(2,1)},...) while((s32[]{:T(128)}, bf16[384,2048]{1,0:T(8,128)(2,1)S(1)}, ...), condition=%wide.region_2.3_spmd.clone, body=%wide.region_0.2_spmd.clone.sunk | while | flops 403374080 | bytes 17957212 | solution.py:43
  2.3 0.2 copy.11
  2.5 3.1 %collective-permute-start = (bf16[384,2048]{1,0:T(8,128)(2,1)S(1)}, bf16[384,2048]{1,0:T(8,128)(2,1)S(1)}, u32[]{:S(2)}, u32[]{:S(2)}) collective-permute-start(bf16[384,2048]{1,0:T(8,128)(2,1)S(1)} %copy.11), channel_id=1, source_target_pairs={{12,0},{0,4},{4,8},{8,12},{13,1},{1,5},{5,9},{9,13},{14,2},{2,6},{... | collective-permute-start | bytes 4718600 | tf_op jit(solution)/shard_map/while/body/eval_jaxpr/ppermute | solution.py:10
  5.6 1.6 %fusion.20 = f32[128,384]{1,0:T(8,128)S(1)} fusion(bf16[128,2048]{1,0:T(8,128)(2,1)} %get-tuple-element.262, bf16[384,2048]{1,0:T(8,128)(2,1)S(1)} %copy.11), kind=kOutput, calls=%fused_computation.10.clone.1 | convolution fusion | flops 201326592 | bytes 2293760 | tf_op jit(solution)/shard_map/while/body/eval_jaxpr/dot_general | solution.py:26
  7.2 9.0 %all-gather.4 = f32[512,384]{1,0:T(8,128)} all-gather(f32[128,384]{1,0:T(8,128)S(1)} %fusion.20), channel_id=2, replica_groups=mesh['kpt'=2,'pert'=4,'pw'=4] {'pw'}, dimensions={0}, use_global_device_ids=true | all-gather | bytes 983040 | tf_op jit(solution)/shard_map/while/body/eval_jaxpr/all_gather | solution.py:29
  16.3 1.2 reduce_sum.28
  17.5 0.7 constant_dynamic-update-slice_fusion.3
  18.2 1.4 %convolution_add_fusion.3 = f32[128,2048]{1,0:T(8,128)} fusion(bf16[384,2048]{1,0:T(8,128)(2,1)S(1)} %copy.11, f32[128,2048]{1,0:T(8,128)} %get-tuple-element.248, pred[]{:T(512)S(6)} %compare.5, f32[128,384]{1,0:T(8,128)S(1)} %reduce_sum.28), kind=kOutput, calls=%fused_computation.clone.1 | convolution fusion | flops 201900032 | bytes 3866625 | tf_op jit(solution)/shard_map/while/body/eval_jaxpr/dot_general | solution.py:32
  19.6 22.4 %collective-permute-done = bf16[384,2048]{1,0:T(8,128)(2,1)S(1)} collective-permute-done((bf16[384,2048]{1,0:T(8,128)(2,1)S(1)}, bf16[384,2048]{1,0:T(8,128)(2,1)S(1)}, u32[]{:S(2)}, u32[]{:S(2)}) %collective-permute-start) | collective-permute-done | bytes 1572896 | tf_op jit(solution)/shard_map/while/body/eval_jaxpr/ppermute | solution.py:10
  42.0 0.2 copy.11
  42.2 0.1 collective-permute-start
  42.3 1.6 %fusion.20 = f32[128,384]{1,0:T(8,128)S(1)} fusion(bf16[128,2048]{1,0:T(8,128)(2,1)} %get-tuple-element.262, bf16[384,2048]{1,0:T(8,128)(2,1)S(1)} %copy.11), kind=kOutput, calls=%fused_computation.10.clone.1 | convolution fusion | flops 201326592 | bytes 2293760 | tf_op jit(solution)/shard_map/while/body/eval_jaxpr/dot_general | solution.py:26
  43.9 9.0 %all-gather.4 = f32[512,384]{1,0:T(8,128)} all-gather(f32[128,384]{1,0:T(8,128)S(1)} %fusion.20), channel_id=2, replica_groups=mesh['kpt'=2,'pert'=4,'pw'=4] {'pw'}, dimensions={0}, use_global_device_ids=true | all-gather | bytes 983040 | tf_op jit(solution)/shard_map/while/body/eval_jaxpr/all_gather | solution.py:29
  53.0 1.2 reduce_sum.28
  54.2 0.7 constant_dynamic-update-slice_fusion.3
  54.9 2.6 %convolution_add_fusion.3 = f32[128,2048]{1,0:T(8,128)} fusion(bf16[384,2048]{1,0:T(8,128)(2,1)S(1)} %copy.11, f32[128,2048]{1,0:T(8,128)} %get-tuple-element.248, pred[]{:T(512)S(6)} %compare.5, f32[128,384]{1,0:T(8,128)S(1)} %reduce_sum.28), kind=kOutput, calls=%fused_computation.clone.1 | convolution fusion | flops 201900032 | bytes 3866625 | tf_op jit(solution)/shard_map/while/body/eval_jaxpr/dot_general | solution.py:32
  57.5 22.1 %collective-permute-done = bf16[384,2048]{1,0:T(8,128)(2,1)S(1)} collective-permute-done((bf16[384,2048]{1,0:T(8,128)(2,1)S(1)}, bf16[384,2048]{1,0:T(8,128)(2,1)S(1)}, u32[]{:S(2)}, u32[]{:S(2)}) %collective-permute-start) | collective-permute-done | bytes 1572896 | tf_op jit(solution)/shard_map/while/body/eval_jaxpr/ppermute | solution.py:10
  79.6 0.2 copy.11
  79.8 0.1 collective-permute-start
  79.9 1.6 %fusion.20 = f32[128,384]{1,0:T(8,128)S(1)} fusion(bf16[128,2048]{1,0:T(8,128)(2,1)} %get-tuple-element.262, bf16[384,2048]{1,0:T(8,128)(2,1)S(1)} %copy.11), kind=kOutput, calls=%fused_computation.10.clone.1 | convolution fusion | flops 201326592 | bytes 2293760 | tf_op jit(solution)/shard_map/while/body/eval_jaxpr/dot_general | solution.py:26
  81.5 8.8 %all-gather.4 = f32[512,384]{1,0:T(8,128)} all-gather(f32[128,384]{1,0:T(8,128)S(1)} %fusion.20), channel_id=2, replica_groups=mesh['kpt'=2,'pert'=4,'pw'=4] {'pw'}, dimensions={0}, use_global_device_ids=true | all-gather | bytes 983040 | tf_op jit(solution)/shard_map/while/body/eval_jaxpr/all_gather | solution.py:29
  90.3 1.2 reduce_sum.28
  91.5 0.7 constant_dynamic-update-slice_fusion.3
  92.2 2.6 %convolution_add_fusion.3 = f32[128,2048]{1,0:T(8,128)} fusion(bf16[384,2048]{1,0:T(8,128)(2,1)S(1)} %copy.11, f32[128,2048]{1,0:T(8,128)} %get-tuple-element.248, pred[]{:T(512)S(6)} %compare.5, f32[128,384]{1,0:T(8,128)S(1)} %reduce_sum.28), kind=kOutput, calls=%fused_computation.clone.1 | convolution fusion | flops 201900032 | bytes 3866625 | tf_op jit(solution)/shard_map/while/body/eval_jaxpr/dot_general | solution.py:32
  94.9 21.4 %collective-permute-done = bf16[384,2048]{1,0:T(8,128)(2,1)S(1)} collective-permute-done((bf16[384,2048]{1,0:T(8,128)(2,1)S(1)}, bf16[384,2048]{1,0:T(8,128)(2,1)S(1)}, u32[]{:S(2)}, u32[]{:S(2)}) %collective-permute-start) | collective-permute-done | bytes 1572896 | tf_op jit(solution)/shard_map/while/body/eval_jaxpr/ppermute | solution.py:10
  116.3 1.6 %convolution_bitcast_fusion = f32[128,384]{0,1:T(8,128)S(1)} fusion(bf16[384,2048]{1,0:T(8,128)(2,1)S(1)} %get-tuple-element.160, bf16[1,128,2048]{2,1,0:T(8,128)(2,1)} %bitcast.28), kind=kOutput, calls=%fused_computation.6 | convolution fusion | flops 201326592 | bytes 2293760 | tf_op jit(solution)/shard_map/dot_general | solution.py:26
  118.0 8.6 %all-gather.1 = f32[512,384]{0,1:T(8,128)} all-gather(f32[128,384]{0,1:T(8,128)S(1)} %convolution_bitcast_fusion), channel_id=3, replica_groups=mesh['kpt'=2,'pert'=4,'pw'=4] {'pw'}, dimensions={0}, use_global_device_ids=true | all-gather | bytes 983040 | tf_op jit(solution)/shard_map/all_gather | solution.py:29
  126.6 0.0 copy-start.1
  126.6 0.0 copy-start.2
  126.6 2.4 %reshape.22 = f32[4,128,384]{1,0,2:T(4,128)} reshape(f32[512,384]{0,1:T(8,128)} %all-gather.1) | data formatting | bytes 1572864 | tf_op jit(solution)/shard_map/all_gather | solution.py:29
  129.0 1.6 %reduce_sum.25 = f32[128,384]{0,1:T(8,128)S(1)} reduce(f32[4,128,384]{1,0,2:T(4,128)} %reshape.22, f32[]{:T(128)} %constant.93.clone.1), dimensions={0}, to_apply=%region_3.4 | reduce | flops 147456 | bytes 983044 | tf_op jit(solution)/shard_map/reduce_sum | solution.py:30
  130.6 0.1 copy.4
  130.7 0.7 constant_dynamic-update-slice_fusion.1
  131.4 0.0 copy-done.1
  131.4 0.0 copy-done.2
  131.4 1.4 %fusion.2 = f32[1,128,2048]{2,1,0:T(8,128)} fusion(f32[128,2048]{1,0:T(8,128)S(1)} %copy-done.1, bf16[384,2048]{1,0:T(8,128)(2,1)S(1)} %get-tuple-element.160, f32[128,384]{0,1:T(8,128)S(1)} %reduce_sum.25, bf16[1,128,2048]{2,1,0:T(8,128)(2,1)S(1)} %bitcast.29), kind=kOutput, calls=%fused_computation.5 | convolution fusion | flops 202162176 | bytes 4390912 | tf_op jit(solution)/shard_map/dot_general | solution.py:32
  (1 shorter events, 0.0 us)
Async XLA Ops:
  0.6 1.7 %copy-start = (bf16[384,2048]{1,0:T(8,128)(2,1)S(1)}, bf16[384,2048]{1,0:T(8,128)(2,1)}, u32[]{:S(2)}) copy-start(bf16[384,2048]{1,0:T(8,128)(2,1)} %param.4) | copy-start | bytes 4718596
  2.5 39.5 %collective-permute-start = (bf16[384,2048]{1,0:T(8,128)(2,1)S(1)}, bf16[384,2048]{1,0:T(8,128)(2,1)S(1)}, u32[]{:S(2)}, u32[]{:S(2)}) collective-permute-start(bf16[384,2048]{1,0:T(8,128)(2,1)S(1)} %copy.11), channel_id=1, source_target_pairs={{12,0},{0,4},{4,8},{8,12},{13,1},{1,5},{5,9},{9,13},{14,2},{2,6},{... | collective-permute-start | bytes 4718600 | tf_op jit(solution)/shard_map/while/body/eval_jaxpr/ppermute | solution.py:10
  42.2 37.4 %collective-permute-start = (bf16[384,2048]{1,0:T(8,128)(2,1)S(1)}, bf16[384,2048]{1,0:T(8,128)(2,1)S(1)}, u32[]{:S(2)}, u32[]{:S(2)}) collective-permute-start(bf16[384,2048]{1,0:T(8,128)(2,1)S(1)} %copy.11), channel_id=1, source_target_pairs={{12,0},{0,4},{4,8},{8,12},{13,1},{1,5},{5,9},{9,13},{14,2},{2,6},{... | collective-permute-start | bytes 4718600 | tf_op jit(solution)/shard_map/while/body/eval_jaxpr/ppermute | solution.py:10
  79.8 36.6 %collective-permute-start = (bf16[384,2048]{1,0:T(8,128)(2,1)S(1)}, bf16[384,2048]{1,0:T(8,128)(2,1)S(1)}, u32[]{:S(2)}, u32[]{:S(2)}) collective-permute-start(bf16[384,2048]{1,0:T(8,128)(2,1)S(1)} %copy.11), channel_id=1, source_target_pairs={{12,0},{0,4},{4,8},{8,12},{13,1},{1,5},{5,9},{9,13},{14,2},{2,6},{... | collective-permute-start | bytes 4718600 | tf_op jit(solution)/shard_map/while/body/eval_jaxpr/ppermute | solution.py:10
  126.6 4.9 %copy-start.1 = (f32[128,2048]{1,0:T(8,128)S(1)}, f32[128,2048]{1,0:T(8,128)}, u32[]{:S(2)}) copy-start(f32[128,2048]{1,0:T(8,128)} %get-tuple-element.161) | copy-start | bytes 3145732
  126.6 4.9 %copy-start.2 = (bf16[128,2048]{1,0:T(8,128)(2,1)S(1)}, bf16[128,2048]{1,0:T(8,128)(2,1)}, u32[]{:S(2)}) copy-start(bf16[128,2048]{1,0:T(8,128)(2,1)} %get-tuple-element.273) | copy-start | bytes 1572868
